TPU v7x, 512 devices: a whole 4x4x16 slice. The times are simulated.
512 devices in a mesh: section: 32 (over y, x, core), ctx: 16 (over z).
Axes of the slice: x: 4, y: 4, z: 16, core: 2. Of those that a mesh axis runs over, the one named last changes fastest.
Arguments:
- streams: bfloat16 [32, 2048, 5120], P('section', 'ctx'), may hold values from -6 to 6
- conv_weight: bfloat16 [32, 4, 5120], P('section'), may hold values from -3 to 3
- beta_logit: float32 [32, 2048, 16], P('section', 'ctx'), may hold values from -12 to 3
- gate_log: float32 [32, 2048, 8], P('section', 'ctx'), may hold values from -2 to 0
- norm_gain: float32 [32, 1024], P('section'), may hold values from 0.25 to 1.75
- w_out: bfloat16 [32, 1024, 2048], P('section', None, 'ctx'), may hold values from -0.1875 to 0.1875
Outputs:
- handed: bfloat16 [32, 2048, 2048], P('section', 'ctx')
All inputs are finite; a program needn't handle non-finite values.
Results may differ from a plain program's by a relative error of at most 0.0049.
Values may be sent and summed in bfloat16 or wider, within the bound.
A program may use at most 128 MiB of HBM per device.

v0:
```python
import jax
import jax.numpy as jnp
from jax import lax
from jax.sharding import PartitionSpec as P

HEAD_TOTAL = 8
HK = 128
STEPS = 2
CONV = 4
SPAN = 128


highest = lax.Precision.HIGHEST


def shifted(value, axis, steps):
    count = lax.axis_size(axis)
    first, last = (max(0, -steps), min(count, count - steps))
    return lax.ppermute(value, axis, [(source, source + steps) for source in range(first, last)])


def entering(value, axis, join, neutral):
    count, mine = (lax.axis_size(axis), lax.axis_index(axis))
    pieces = jax.tree.map(lambda part: lax.all_gather(part, axis), value)
    total = jax.tree.map(
        lambda part, zero: jnp.full_like(part, 0) + jnp.asarray(zero, part.dtype), value, neutral
    )

    def turn(position, total):
        longer = join(total, jax.tree.map(lambda part: part[position], pieces))
        return jax.tree.map(lambda new, old: jnp.where(position < mine, new, old), longer, total)

    return lax.fori_loop(0, count - 1, turn, total)


def passed_along(value, axis, steps):
    count = lax.axis_size(axis)
    pairs = [(source, (source + steps) % count) for source in range(count)]
    return lax.ppermute(value, axis, pairs)


def mix_taps(extended, tap_weights):
    tok_count = extended.shape[0] - tap_weights.shape[0] + 1
    summed = jnp.zeros((tok_count, extended.shape[1]), jnp.float32)
    for offset in range(tap_weights.shape[0]):
        summed = summed + tap_weights[offset].astype(jnp.float32) * extended[
            offset : offset + tok_count
        ].astype(jnp.float32)
    return jax.nn.silu(summed)


def unit_rows(vectors):
    return vectors * lax.rsqrt(jnp.sum(vectors * vectors, axis=-1, keepdims=True) + 1e-06)


def head_major(active, beta_logit, gate_log):
    tok_count = active.shape[0]
    head_width = HEAD_TOTAL * HK
    queries = unit_rows(active[:, :head_width].reshape(tok_count, HEAD_TOTAL, HK)).transpose(
        1, 0, 2
    )
    keys_all = unit_rows(
        active[:, head_width : (1 + STEPS) * head_width].reshape(tok_count, STEPS, HEAD_TOTAL, HK)
    )
    keys_all = keys_all.transpose(2, 0, 1, 3).reshape(HEAD_TOTAL, tok_count * STEPS, HK)
    values_all = active[:, (1 + STEPS) * head_width :].reshape(tok_count, STEPS, HEAD_TOTAL, HK)
    values_all = values_all.transpose(2, 0, 1, 3).reshape(HEAD_TOTAL, tok_count * STEPS, HK)
    step_size = (
        jax.nn.sigmoid(beta_logit.reshape(tok_count, STEPS, HEAD_TOTAL))
        .transpose(2, 0, 1)
        .reshape(HEAD_TOTAL, tok_count * STEPS)
    )
    opening = (lax.broadcasted_iota(jnp.int32, (1, STEPS, 1), 1) == 0).astype(gate_log.dtype)
    log_gate = (
        (gate_log[:, None, :] * opening).transpose(2, 0, 1).reshape(HEAD_TOTAL, tok_count * STEPS)
    )
    return (queries, keys_all, values_all, step_size, log_gate)


def span_terms(queries, keys_all, values_all, step_size, log_gate):
    head_count, virtual, head_dim = keys_all.shape
    blocks = virtual // SPAN
    per_block = SPAN // STEPS
    queries = queries.reshape(head_count, blocks, per_block, head_dim)
    keys_all = keys_all.reshape(head_count, blocks, SPAN, head_dim)
    values_all = values_all.reshape(head_count, blocks, SPAN, head_dim)
    step_size = step_size.reshape(head_count, blocks, SPAN)
    cumulate = jnp.cumsum(log_gate.reshape(head_count, blocks, SPAN), axis=-1)
    query_log = cumulate[..., STEPS - 1 :: STEPS]
    row_index = lax.broadcasted_iota(jnp.int32, (SPAN, SPAN), 0)
    col_index = lax.broadcasted_iota(jnp.int32, (SPAN, SPAN), 1)
    strict = col_index < row_index
    spread = cumulate[..., :, None] - cumulate[..., None, :]
    damping = jnp.where(strict, jnp.exp(jnp.where(strict, spread, 0.0)), 0.0)
    key_inner = jnp.einsum("hcid,hcjd->hcij", keys_all, keys_all, precision=highest)
    unit_lower = (
        jnp.eye(SPAN, dtype=key_inner.dtype) + step_size[..., :, None] * damping * key_inner
    )
    right_sides = jnp.concatenate(
        [step_size[..., None] * values_all, (step_size * jnp.exp(cumulate))[..., None] * keys_all],
        axis=-1,
    )
    solved = jax.scipy.linalg.solve_triangular(
        unit_lower, right_sides, lower=True, unit_diagonal=True
    )
    value_part = solved[..., :head_dim]
    key_part = solved[..., head_dim:]
    to_end = keys_all * jnp.exp(cumulate[..., -1:] - cumulate)[..., None]
    carried = jnp.exp(cumulate[..., -1])[..., None, None] * jnp.eye(head_dim, dtype=key_inner.dtype)
    carried = carried - jnp.einsum("hcid,hcie->hcde", to_end, key_part, precision=highest)
    written = jnp.einsum("hcid,hcie->hcde", to_end, value_part, precision=highest)
    query_row = lax.broadcasted_iota(jnp.int32, (per_block, SPAN), 0) * STEPS + STEPS - 1
    query_col = lax.broadcasted_iota(jnp.int32, (per_block, SPAN), 1)
    allowed = query_col <= query_row
    query_spread = query_log[..., :, None] - cumulate[..., None, :]
    query_damping = jnp.where(allowed, jnp.exp(jnp.where(allowed, query_spread, 0.0)), 0.0)
    scores = jnp.einsum("hcpd,hcid->hcpi", queries, keys_all, precision=highest) * query_damping
    direct = jnp.einsum("hcpi,hcie->hcpe", scores, value_part, precision=highest)
    reach_map = queries * jnp.exp(query_log)[..., None] - jnp.einsum(
        "hcpi,hcie->hcpe", scores, key_part, precision=highest
    )
    return (
        jnp.moveaxis(carried, 1, 0),
        jnp.moveaxis(written, 1, 0),
        jnp.moveaxis(direct, 1, 0),
        jnp.moveaxis(reach_map, 1, 0),
    )


def advance(state_now, piece_terms):
    carried, written, direct, reach_map = piece_terms
    span_out = direct + jnp.einsum("hpd,hde->hpe", reach_map, state_now, precision=highest)
    state_now = jnp.einsum("hde,hef->hdf", carried, state_now, precision=highest) + written
    return (state_now, span_out)


def normalize(outputs, norm_gain):
    tok_count = outputs.shape[0]
    inverse_rms = lax.rsqrt(jnp.mean(outputs * outputs, axis=-1, keepdims=True) + 1e-05)
    return (
        (outputs * inverse_rms * norm_gain.reshape(HEAD_TOTAL, HK))
        .reshape(tok_count, HEAD_TOTAL * HK)
        .astype(jnp.bfloat16)
    )


def combine_pairs(earlier_pair, later_pair):
    first_map, first_add = earlier_pair
    second_map, second_add = later_pair
    joined_map = jnp.einsum("hde,hef->hdf", second_map, first_map, precision=highest)
    joined_add = jnp.einsum("hde,hef->hdf", second_map, first_add, precision=highest) + second_add
    return (joined_map, joined_add)


def compose_step(carried_in, piece_terms):
    so_far, added_state = carried_in
    next_map = jnp.einsum("hde,hef->hdf", piece_terms[0], so_far, precision=highest)
    next_add = (
        jnp.einsum("hde,hef->hdf", piece_terms[0], added_state, precision=highest) + piece_terms[1]
    )
    return ((next_map, next_add), None)


def on_device(streams, conv_weight, beta_logit, gate_log, norm_gain, w_out):
    own_rows = streams[0]
    tok_count = own_rows.shape[0]
    rim_rows = shifted(own_rows[tok_count - (CONV - 1) :], "ctx", 1)
    active = mix_taps(jnp.concatenate([rim_rows, own_rows], axis=0), conv_weight[0])
    span_parts = span_terms(*head_major(active, beta_logit[0], gate_log[0]))
    identity_map = jnp.broadcast_to(jnp.eye(HK, dtype=jnp.float32), (HEAD_TOTAL, HK, HK))
    nothing = jnp.zeros((HEAD_TOTAL, HK, HK), jnp.float32)
    (total_map, total_add), _ = lax.scan(compose_step, (identity_map, nothing), span_parts)
    _, incoming = entering((total_map, total_add), "ctx", combine_pairs, (identity_map, nothing))
    _, outputs = lax.scan(advance, incoming, span_parts)
    outputs = outputs.transpose(0, 2, 1, 3).reshape(tok_count, HEAD_TOTAL, HK)
    normed = normalize(outputs, norm_gain[0])
    local_cols = w_out[0]
    mixed_rows = jnp.dot(
        normed,
        lax.all_gather(local_cols, "ctx", axis=1, tiled=True),
        preferred_element_type=jnp.float32,
    ).astype(jnp.bfloat16)
    return passed_along(mixed_rows[None], "section", 1)


def solution(mesh):
    placed = (
        P("section", "ctx", None),
        P("section", None, None),
        P("section", "ctx", None),
        P("section", "ctx", None),
        P("section", None),
        P("section", None, "ctx"),
    )
    return jax.shard_map(
        on_device, mesh=mesh, in_specs=placed, out_specs=P("section", "ctx", None), check_vma=False
    )
```

profile of v0, /device:TPU:32, one launch (start us, length us, event | category | flops | bytes accessed | tf_op | source)
XLA Modules:
  0.0 527.9 jit_solution(1281271470755481892)
XLA Ops:
  7.6 3.8 collective-permute-start
  22.7 2.4 fusion.43
  25.1 157.9 %custom-call.4 = f32[8,2,1,128,128]{3,4,2,1,0:T(8,128)} custom-call(f32[8,2,1,128,128]{4,3,2,1,0:T(8,128)S(1)} %fusion.43), custom_call_target="InvertDiagBlocksLowerTriangular" | custom-call | tf_op jit(solution)/shard_map/jit(_solve_triangular)/vmap(vmap())/triangular_solve | solution.py:103
  183.0 1.9 broadcast_multiply_fusion
  184.9 2.0 fusion.35
  186.9 2.2 convolution_bitcast_fusion
  189.3 2.2 fusion.39
  191.7 2.9 while.40
  199.0 2.1 convolution_multiply_fusion.1
  204.1 97.6 %all-gather.7.cloned.1.call-done = f32[128,128,128]{2,1,0:T(8,128)} async-done(((f32[8,128,128]{2,1,0:T(8,128)}), f32[128,128,128]{2,1,0:T(8,128)}) %all-gather.7.cloned.1.call-update) | async-done | bytes 8388624 | tf_op jit(solution)/shard_map/all_gather | solution.py:24
  301.7 105.9 %all-gather.9.cloned.1.call-done = f32[128,128,128]{2,1,0:T(8,128)} async-done(((f32[8,128,128]{2,1,0:T(8,128)}), f32[128,128,128]{2,1,0:T(8,128)}) %all-gather.9.cloned.1.call-update) | async-done | bytes 8388624 | tf_op jit(solution)/shard_map/all_gather | solution.py:24
  407.6 29.2 %while.41 = (s32[]{:T(128)}, f32[8,128,128]{2,1,0:T(8,128)S(1)}, s32[]{:T(128)}, f32[16,8,128,128]{3,2,1,0:T(8,128)}, f32[16,8,128,128]{3,2,1,0:T(8,128)}, /*index=5*/s32[]{:T(128)}, s32[]{:T(128)}) while((s32[]{:T(128)}, f32[8,128,128]{2,1,0:T(8,128)S(1)}, s32[]{:T(128)}, f32[16,8,128,128]{3,2,1,0:T(8,128)}, ...), condition=%wide.region_5.6_spmd.clone, body=%wide.region_4.5_spmd.clone.sunk | while | flops 201850880 | bytes 3672671 | solution.py:33
  407.6 1.9 fusion.97
  409.6 1.9 fusion.97
  413.5 1.9 fusion.97
  415.4 1.9 fusion.97
  417.4 1.9 fusion.97
  419.3 1.9 fusion.97
  421.3 1.9 fusion.97
  423.2 1.9 fusion.97
  425.2 1.9 fusion.97
  427.1 1.9 fusion.97
  429.1 1.9 fusion.97
  431.0 1.9 fusion.97
  434.9 1.9 fusion.97
  436.8 6.0 %while.39 = (s32[]{:T(128)}, f32[8,128,128]{2,1,0:T(8,128)S(1)}, f32[2,8,64,128]{3,2,1,0:T(8,128)}, f32[2,8,128,128]{3,2,1,0:T(8,128)S(1)}, f32[2,8,128,128]{3,2...) while((s32[]{:T(128)}, f32[8,128,128]{2,1,0:T(8,128)S(1)}, ...), condition=%wide.region_8.9_spmd, body=%wide.region_7.8_spmd.sunk | while | flops 302186496 | bytes 4458581 | solution.py:174
  436.9 2.3 fusion.89
  439.9 2.3 fusion.89
  445.5 58.0 %all-gather.11.cloned.1.call-done = bf16[1,1024,2048]{2,1,0:T(8,128)(2,1)} async-done(((bf16[1,1024,128]{2,1,0:T(8,128)(2,1)}), bf16[1,1024,2048]{2,1,0:T(8,128)(2,1)}) %all-gather.11.cloned.1.call-update) | async-done | bytes 4194320 | tf_op jit(solution)/shard_map/all_gather | solution.py:180
  503.7 3.0 fusion.32
  506.7 1.9 collective-permute-start.1
  508.7 11.9 %collective-permute-done.1 = bf16[1,128,2048]{2,1,0:T(8,128)(2,1)S(1)} collective-permute-done((bf16[1,128,2048]{2,1,0:T(8,128)(2,1)S(1)}, bf16[1,128,2048]{2,1,0:T(8,128)(2,1)S(1)}, u32[]{:S(2)}, u32[]{:S(2)}) %collective-permute-start.1) | collective-permute-done | bytes 524320 | tf_op jit(solution)/shard_map/ppermute | solution.py:39
  (115 shorter events, 31.8 us)
Async XLA Ops:
  6.5 9.7 %copy-start.7 = (bf16[1,128,5120]{2,1,0:T(8,128)(2,1)S(1)}, bf16[1,128,5120]{2,1,0:T(8,128)(2,1)}, u32[]{:S(2)}) copy-start(bf16[1,128,5120]{2,1,0:T(8,128)(2,1)} %param.12) | copy-start | bytes 3932164
  6.5 295.1 %all-gather.7.cloned.1.call-start = ((), (), s32[]{:S(2)}) async-start(), calls=%async_computation | async-start | bytes 8912896 | tf_op jit(solution)/shard_map/all_gather | solution.py:24
  7.6 8.7 %collective-permute-start = (bf16[3,5120]{1,0:T(4,128)(2,1)S(1)}, bf16[3,5120]{1,0:T(4,128)(2,1)S(1)}, u32[]{:S(2)}, u32[]{:S(2)}) collective-permute-start(bf16[3,5120]{1,0:T(4,128)(2,1)S(1)} %slice_bitcast_fusion.3), channel_id=1, source_target_pairs={{0,1},{1,2},{2,3},{3,4},{4,5},{5,6},{6,7},{7,8},{8,9},{9,10},{10,1... | collective-permute-start | bytes 92168 | tf_op jit(solution)/shard_map/ppermute | solution.py:19
  18.1 1.5 copy-start.6
  21.0 168.3 %copy-start = (f32[8,128,2,128]{3,2,1,0:T(2,128)}, f32[8,128,2,128]{3,2,1,0:T(2,128)S(1)}, u32[]{:S(2)}) copy-start(f32[8,128,2,128]{3,2,1,0:T(2,128)S(1)} %copy.83) | copy-start | bytes 3145732
  183.0 1.9 copy-start.8
  186.9 2.3 copy-start.3
  194.5 0.8 copy-start.2
  194.5 1.0 copy-start.5
  195.4 212.2 %all-gather.9.cloned.1.call-start = ((), (), s32[]{:S(2)}) async-start(), calls=%async_computation.1 | async-start | bytes 8912896 | tf_op jit(solution)/shard_map/all_gather | solution.py:24
  196.1 307.4 %all-gather.11.cloned.1.call-start = ((), (), s32[]{:S(2)}) async-start(), calls=%async_computation.2 | async-start | bytes 4456448 | tf_op jit(solution)/shard_map/all_gather | solution.py:180
  197.1 1.9 copy-start.1
  198.5 2.7 copy-start.4
  436.8 66.9 %copy-start.9 = (f32[1,1024]{1,0:T(1,128)S(1)}, f32[1,1024]{1,0:T(1,128)}, u32[]{:S(2)}) copy-start(f32[1,1024]{1,0:T(1,128)} %param.16) | copy-start | bytes 12292
  506.7 13.8 %collective-permute-start.1 = (bf16[1,128,2048]{2,1,0:T(8,128)(2,1)S(1)}, bf16[1,128,2048]{2,1,0:T(8,128)(2,1)S(1)}, u32[]{:S(2)}, u32[]{:S(2)}) collective-permute-start(bf16[1,128,2048]{2,1,0:T(8,128)(2,1)S(1)} %fusion.32), channel_id=1, source_target_pairs={{0,16},{16,32},{32,48},{48,64},{64,80},{80,96},{96,112},{112,128},... | collective-permute-start | bytes 1572872 | tf_op jit(solution)/shard_map/ppermute | solution.py:39
Sparse Core Ops, SparseCore 0:
  195.5 106.1 all-gather.6
  303.8 103.7 all-gather.8
  409.6 93.8 all-gather.10
where the time goes:
time: 529 us; the launch traced here: 528 us
  waiting for transfers between devices  275 us (52%)
  other arithmetic  167 us (32%)
  matrix products  53.5 us (10%)
  between operations  13.6 us (3%)
  local copies, waits for them, and re-layouts  12.2 us (2%)
  starting transfers between devices  6.05 us (1%)
    all_gather x2, waiting for transfers between devices, entering(): pieces = jax.tree.map(lambda part: lax.all_gather(part, axis), value)  203 us
    another operation x2, other arithmetic, span_terms(): jax.scipy.linalg.solve_triangular(unit_lower, right_sides, lower=True, un...  158 us
    all_gather x1, waiting for transfers between devices, on_device(): lax.all_gather(local_cols, 'ctx', axis=1, tiled=True)  58 us
    dot_general x15, matrix products, combine_pairs(): jnp.einsum('hde,hef->hdf', second_map, first_add, precision=highest)  28.1 us
    ppermute x1, waiting for transfers between devices, passed_along(): return lax.ppermute(value, axis, pairs)  11.9 us
  transfers between devices with their start and end apart: 5, of which 5 were waited for; matrix products, arithmetic and copies ran while one was open for 9% of the time, Pallas kernels for 0%

commit v1 on v0

v1 whole, which is shorter than its diff:
```python
import functools

import jax
import jax.numpy as jnp
from jax import lax
from jax.experimental import pallas as pl
from jax.experimental.pallas import tpu as pltpu
from jax.sharding import PartitionSpec as P

HEAD_TOTAL = 8
HK = 128
STEPS = 2
CONV = 4
TOK = 128
PAIR = 2
MESH = pl.DeviceIdType.MESH
highest = lax.Precision.HIGHEST

NN = (((1,), (0,)), ((), ()))
NT = (((1,), (1,)), ((), ()))
TN = (((0,), (0,)), ((), ()))


def split(a):
    high = a.astype(jnp.bfloat16)
    return high, (a - high.astype(jnp.float32)).astype(jnp.bfloat16)


def dot(a, b, dims=NN):
    return lax.dot_general(a, b, dims, preferred_element_type=jnp.float32)


def dot3(a, b, dims=NN):
    (ah, al), (bh, bl) = a, b
    return dot(ah, bh, dims) + (dot(ah, bl, dims) + dot(al, bh, dims))


def unit_rows(vectors):
    return vectors * lax.rsqrt(jnp.sum(vectors * vectors, axis=-1, keepdims=True) + 1e-06)


def local_terms(heads):
    both = STEPS * TOK
    row = lax.broadcasted_iota(jnp.int32, (both, both), 0)
    col = lax.broadcasted_iota(jnp.int32, (both, both), 1)
    row_tok, col_tok = row & (TOK - 1), col & (TOK - 1)
    tok_row = lax.broadcasted_iota(jnp.int32, (TOK, TOK), 0)
    tok_col = lax.broadcasted_iota(jnp.int32, (TOK, TOK), 1)
    before = (col_tok < row_tok) | ((col_tok == row_tok) & (col < row))
    keys, sizes, inner, damp = [], [], [], []
    for q, k0, k1, v0, v1, b0, b1, c_col, c_row in heads:
        key = jnp.concatenate([k0, k1], axis=0)
        keys.append(key)
        sizes.append(jnp.concatenate([b0, b1], axis=0))
        kept = jnp.where(tok_col <= tok_row, jnp.exp(jnp.minimum(c_col - c_row, 0.0)), 0.0)
        damp.append(jnp.concatenate([kept, kept], axis=1))
    key_parts = [split(key) for key in keys]
    lower = []
    for parts, size, kept in zip(key_parts, sizes, damp):
        grid = dot3(parts, parts, NT)
        wide = jnp.concatenate([kept, kept], axis=0)
        lower.append(jnp.where(before, size * wide * grid, 0.0))
    eye = (row == col).astype(jnp.float32)
    same = row_tok == col_tok
    inverse = [eye - jnp.where(same, m, 0.0) for m in lower]
    shift = 0
    while (1 << shift) < TOK:
        joined = ((row_tok >> (shift + 1)) == (col_tok >> (shift + 1))) & (
            (row_tok >> shift) != (col_tok >> shift)
        )
        inv_parts = [split(x) for x in inverse]
        crosses = [split(jnp.where(joined, m, 0.0)) for m in lower]
        halves = [split(dot3(c, x)) for c, x in zip(crosses, inv_parts)]
        inverse = [x - dot3(p, y) for x, p, y in zip(inverse, inv_parts, halves)]
        shift += 1
    results = []
    for (q, k0, k1, v0, v1, b0, b1, c_col, c_row), key, parts, kept, x in zip(
        heads, keys, key_parts, damp, inverse
    ):
        grown = jnp.exp(c_col)
        right = jnp.concatenate(
            [
                jnp.concatenate([b0 * v0, b1 * v1], axis=0),
                jnp.concatenate([(b0 * grown) * k0, (b1 * grown) * k1], axis=0),
            ],
            axis=1,
        )
        solved = split(dot3(split(x), split(right)))
        last = c_col[TOK - 1 :, :]
        rest = jnp.exp(last - c_col)
        ends = split(jnp.concatenate([k0 * rest, k1 * rest], axis=0))
        moved = dot3(ends, solved, TN)
        scores = split(dot3(split(q), parts, NT) * kept)
        seen = dot3(scores, solved)
        written, taken = moved[:, :HK], moved[:, HK:]
        direct, reach = seen[:, :HK], q * grown - seen[:, HK:]
        results.append((taken, written, direct, reach, jnp.exp(last)))
    return results


def local_kernel(
    q_ref, k0_ref, k1_ref, v0_ref, v1_ref,
    qr, k0r, k1r, v0r, v1r,
    qw, k0w, k1w, v0w, v1w,
    beta_ref, gate_ref,
    taken_ref, written_ref, direct_ref, reach_ref, keep_ref,
    ext,
):
    first = pl.program_id(0) * PAIR

    def act(x_ref, rim_ref, w_ref):
        ext[8 - (CONV - 1) : 8, :] = rim_ref[...].astype(jnp.float32)
        ext[8:, :] = x_ref[...].astype(jnp.float32)
        summed = jnp.zeros((TOK, PAIR * HK), jnp.float32)
        taps = w_ref[...].astype(jnp.float32)
        for i in range(CONV):
            start = 8 - (CONV - 1) + i
            summed = summed + taps[i : i + 1] * ext[start : start + TOK, :]
        return summed * jax.nn.sigmoid(summed)

    queries = act(q_ref, qr, qw)
    key_0, key_1 = act(k0_ref, k0r, k0w), act(k1_ref, k1r, k1w)
    value_0, value_1 = act(v0_ref, v0r, v0w), act(v1_ref, v1r, v1w)
    tok_row = lax.broadcasted_iota(jnp.int32, (TOK, TOK), 0)
    tok_col = lax.broadcasted_iota(jnp.int32, (TOK, TOK), 1)
    ones = (tok_col <= tok_row).astype(jnp.float32)
    gates = gate_ref[...]
    c_cols = lax.dot_general(ones, gates, NN, precision=highest, preferred_element_type=jnp.float32)
    c_rows = lax.dot_general(
        gates, ones, (((0,), (1,)), ((), ())), precision=highest, preferred_element_type=jnp.float32
    )
    betas = jax.nn.sigmoid(beta_ref[...])

    def column(values, which):
        lane = lax.broadcasted_iota(jnp.int32, values.shape, 1)
        return jnp.sum(jnp.where(lane == which, values, 0.0), axis=1, keepdims=True)

    def picked_row(values, which):
        lane = lax.broadcasted_iota(jnp.int32, values.shape, 0)
        return jnp.sum(jnp.where(lane == which, values, 0.0), axis=0, keepdims=True)

    heads = []
    for p in range(PAIR):
        at = slice(p * HK, (p + 1) * HK)
        heads.append(
            (
                unit_rows(queries[:, at]),
                unit_rows(key_0[:, at]),
                unit_rows(key_1[:, at]),
                value_0[:, at],
                value_1[:, at],
                column(betas, first + p),
                column(betas, HEAD_TOTAL + first + p),
                column(c_cols, first + p),
                picked_row(c_rows, first + p),
            )
        )
    for p, (taken, written, direct, reach, keep) in enumerate(local_terms(heads)):
        taken_ref[p] = taken
        written_ref[p] = written
        direct_ref[p] = direct
        reach_ref[p] = reach
        keep_ref[p] = jnp.broadcast_to(keep, (8, HK))


def local_call(rows, rim, taps, beta, gate):
    groups = HEAD_TOTAL // PAIR
    width = PAIR * HK

    def specs(height):
        return [
            pl.BlockSpec((height, width), functools.partial(lambda n, g: (0, n * groups + g), n))
            for n in range(1 + 2 * STEPS)
        ]

    square = jax.ShapeDtypeStruct((HEAD_TOTAL, HK, HK), jnp.float32)
    square_spec = pl.BlockSpec((PAIR, HK, HK), lambda g: (g, 0, 0))
    return pl.pallas_call(
        local_kernel,
        grid=(groups,),
        in_specs=specs(TOK)
        + specs(CONV - 1)
        + specs(CONV)
        + [
            pl.BlockSpec((TOK, STEPS * HEAD_TOTAL), lambda g: (0, 0)),
            pl.BlockSpec((TOK, HEAD_TOTAL), lambda g: (0, 0)),
        ],
        out_specs=[square_spec] * 4 + [pl.BlockSpec((PAIR, 8, HK), lambda g: (g, 0, 0))],
        out_shape=[square] * 4 + [jax.ShapeDtypeStruct((HEAD_TOTAL, 8, HK), jnp.float32)],
        scratch_shapes=[pltpu.VMEM((TOK + 8, width), jnp.float32)],
        name="local_terms",
        cost_estimate=pl.CostEstimate(
            flops=8 * 50 * 2 * 256**3, bytes_accessed=4_000_000, transcendentals=1_000_000
        ),
    )(*([rows] * 5 + [rim] * 5 + [taps] * 5), beta, gate)


def chain_kernel(
    count, taken_ref, written_ref, direct_ref, reach_ref, keep_ref, gain_ref, normed_ref,
    entering, leaving, send_sem, recv_sem,
):
    mine = lax.axis_index("ctx")
    after, prior = lax.rem(mine + 1, count), lax.rem(mine + count - 1, count)
    barrier = pltpu.get_barrier_semaphore()
    for other in (after, prior):
        pl.semaphore_signal(barrier, inc=1, device_id={"ctx": other}, device_id_type=MESH)
    pl.semaphore_wait(barrier, 2)

    def hop(h):
        return pltpu.make_async_remote_copy(
            src_ref=leaving.at[h],
            dst_ref=entering.at[h],
            send_sem=send_sem.at[h],
            recv_sem=recv_sem.at[h],
            device_id={"ctx": after},
            device_id_type=MESH,
        )

    @pl.when(mine == 0)
    def _():
        entering[...] = jnp.zeros_like(entering)

    for h in range(HEAD_TOTAL):
        @pl.when(mine > 0)
        def _():
            hop(h).wait_recv()

        state = entering[h]
        parts = split(state)
        step = keep_ref[h][:1] * state - dot3(split(taken_ref[h]), parts) + written_ref[h]

        @pl.when(mine < count - 1)
        def _():
            leaving[h] = step
            hop(h).start()

        out = direct_ref[h] + dot3(split(reach_ref[h]), parts)
        scale = lax.rsqrt(jnp.mean(out * out, axis=-1, keepdims=True) + 1e-05)
        at = slice(h * HK, (h + 1) * HK)
        normed_ref[:, at] = (out * scale * gain_ref[:, at]).astype(jnp.bfloat16)

    @pl.when(mine < count - 1)
    def _():
        for h in range(HEAD_TOTAL):
            hop(h).wait_send()


def chain_call(count, terms, gain):
    whole = pl.BlockSpec(memory_space=pltpu.VMEM)
    return pl.pallas_call(
        functools.partial(chain_kernel, count),
        in_specs=[whole] * 6,
        out_specs=whole,
        out_shape=jax.ShapeDtypeStruct((TOK, HEAD_TOTAL * HK), jnp.bfloat16),
        scratch_shapes=[
            pltpu.VMEM((HEAD_TOTAL, HK, HK), jnp.float32),
            pltpu.VMEM((HEAD_TOTAL, HK, HK), jnp.float32),
            pltpu.SemaphoreType.DMA((HEAD_TOTAL,)),
            pltpu.SemaphoreType.DMA((HEAD_TOTAL,)),
        ],
        compiler_params=pltpu.CompilerParams(collective_id=0, has_side_effects=True),
        name="state_chain",
        cost_estimate=pl.CostEstimate(
            flops=50_000_000_000, bytes_accessed=3_000_000, transcendentals=0
        ),
    )(*terms, gain)


def on_device(streams, conv_weight, beta_logit, gate_log, norm_gain, w_out):
    count = lax.axis_size("ctx")
    sections = lax.axis_size("section")
    rows = streams[0]
    rim = lax.ppermute(
        rows[rows.shape[0] - (CONV - 1) :], "ctx", [(s, s + 1) for s in range(count - 1)]
    )
    columns = lax.all_gather(w_out[0], "ctx", axis=1, tiled=True)
    terms = local_call(rows, rim, conv_weight[0], beta_logit[0], gate_log[0])
    normed = chain_call(count, terms, norm_gain)
    mixed = jnp.dot(normed, columns, preferred_element_type=jnp.float32).astype(jnp.bfloat16)
    return lax.ppermute(
        mixed[None], "section", [(s, (s + 1) % sections) for s in range(sections)]
    )


def solution(mesh):
    placed = (
        P("section", "ctx", None),
        P("section", None, None),
        P("section", "ctx", None),
        P("section", "ctx", None),
        P("section", None),
        P("section", None, "ctx"),
    )
    return jax.shard_map(
        on_device, mesh=mesh, in_specs=placed, out_specs=P("section", "ctx", None), check_vma=False
    )
```

time: 529 us -> 153 us (0.29)
  the two profiles are of different devices: /device:TPU:32 before, /device:TPU:496 now
where the time goes in v1:
time: 153 us
  Pallas kernels  115 us (75%)
  between operations  13.4 us (9%)
  waiting for transfers between devices  13.2 us (9%)
  local copies, waits for them, and re-layouts  5.16 us (3%)
  starting transfers between devices  3.21 us (2%)
  matrix products  3 us (2%)
    pallas_call x1, Pallas kernels, chain_call(): pl.pallas_call(functools.partial(chain_kernel, count), in_specs=[whole] *...  85.7 us
    pallas_call x1, Pallas kernels, local_call(): pl.pallas_call(local_kernel, grid=(groups,), in_specs=specs(TOK) + specs(...  29 us
    ppermute x1, waiting for transfers between devices, on_device(): lax.ppermute(mixed[None], 'section', [(s, (s + 1) % sections) for s in ra...  10.7 us
    unnamed x5, local copies, waits for them, and re-layouts  4.25 us
  transfers between devices with their start and end apart: 3, of which 2 were waited for; matrix products, arithmetic and copies ran while one was open for 2% of the time, Pallas kernels for 75%

profile of v1, /device:TPU:496, one launch (start us, length us, event | category | flops | bytes accessed | tf_op | source)
XLA Modules:
  0.0 152.8 jit_solution(4774808592775673324)
XLA Ops:
  6.5 0.0 all-gather.3.cloned.1.call-start
  6.5 0.7 all-gather.3.cloned.1.call-update
  7.3 0.9 slice_bitcast_fusion
  8.2 1.3 collective-permute-start
  9.5 1.4 copy.7
  10.9 1.4 copy.8
  12.3 1.8 %collective-permute-done.qr.k0r.k1r.v0r.v1r = bf16[3,5120]{1,0:T(4,128)(2,1)S(1)} collective-permute-done((bf16[3,5120]{1,0:T(4,128)(2,1)S(1)}, bf16[3,5120]{1,0:T(4,128)(2,1)S(1)}, u32[]{:S(2)}, u32[]{:S(2)}) %collective-permute-start) | collective-permute-done | bytes 30752 | tf_op jit(solution)/shard_map/ppermute | solution.py:273
  14.1 0.0 copy-start
  14.1 0.6 copy-done
  14.7 29.0 %local_terms.1 = (f32[8,128,128]{2,1,0:T(8,128)}, f32[8,128,128]{2,1,0:T(8,128)}, f32[8,128,128]{2,1,0:T(8,128)}, f32[8,128,128]{2,1,0:T(8,128)}, f32[8,8,128]{2,1,0:T(8,128)}) custom-call(bf16[128,5120]{1,0:T(8,128)(2,1)} %bitcast.18, bf16[128,5120]{1,0:T(8,128)(2,1)} %bitcast.19, bf16[128,5120]{1,0:T(8,128)(2,1)} %bitcast.20, bf16[128,5120]{1,0:T(8,128)(2,1)} %bitcast.21, ...), custom_call_target="tpu_custom_call" | custom-call | flops 13421772800 | bytes 4000000 | tf_op jit(solution)/shard_map/local_terms/pallas_call | solution.py:178
  43.7 85.7 %state_chain.1 = bf16[128,1024]{1,0:T(8,128)(2,1)} custom-call(f32[8,128,128]{2,1,0:T(8,128)} %get-tuple-element.10.taken_ref, f32[8,128,128]{2,1,0:T(8,128)} %get-tuple-element.11.written_ref, f32[8,128,128]{2,1,0:T(8,128)} %get-tuple-element.12.direct_ref, f32[8,128,128]{2,1,0:T(8,128)} %get-tuple-element.13.reach_ref, ...), custom_call_target="tpu_custom_call" | custom-call | flops 49999998976 | bytes 3000000 | tf_op jit(solution)/shard_map/state_chain/pallas_call | solution.py:250
  129.5 0.0 all-gather.3.cloned.1.call-done
  129.5 3.0 %fusion.5 = bf16[1,128,2048]{2,1,0:T(8,128)(2,1)S(1)} fusion(bf16[128,1024]{1,0:T(8,128)(2,1)} %state_chain.1, bf16[1,1024,2048]{2,1,0:T(8,128)(2,1)} %all-gather.3.cloned.1.call-done), kind=kOutput, calls=%fused_computation.3 | convolution fusion | flops 537133056 | bytes 4980736 | tf_op jit(solution)/shard_map/dot_general | solution.py:279
  132.5 1.9 %collective-permute-start.1 = (bf16[1,128,2048]{2,1,0:T(8,128)(2,1)S(1)}, bf16[1,128,2048]{2,1,0:T(8,128)(2,1)S(1)}, u32[]{:S(2)}, u32[]{:S(2)}) collective-permute-start(bf16[1,128,2048]{2,1,0:T(8,128)(2,1)S(1)} %fusion.5), channel_id=1, source_target_pairs={{0,16},{16,32},{32,48},{48,64},{64,80},{80,96},{96,112},{112,128},... | collective-permute-start | bytes 1572872 | tf_op jit(solution)/shard_map/ppermute | solution.py:280
  134.4 10.7 %collective-permute-done.1 = bf16[1,128,2048]{2,1,0:T(8,128)(2,1)S(1)} collective-permute-done((bf16[1,128,2048]{2,1,0:T(8,128)(2,1)S(1)}, bf16[1,128,2048]{2,1,0:T(8,128)(2,1)S(1)}, u32[]{:S(2)}, u32[]{:S(2)}) %collective-permute-start.1) | collective-permute-done | bytes 524320 | tf_op jit(solution)/shard_map/ppermute | solution.py:280
  145.1 0.8 copy.10
Async XLA Ops:
  6.5 123.0 %all-gather.3.cloned.1.call-start = ((), (), s32[]{:S(2)}) async-start(), calls=%async_computation | async-start | bytes 4456448 | tf_op jit(solution)/shard_map/all_gather | solution.py:276
  8.2 5.9 %collective-permute-start = (bf16[3,5120]{1,0:T(4,128)(2,1)S(1)}, bf16[3,5120]{1,0:T(4,128)(2,1)S(1)}, u32[]{:S(2)}, u32[]{:S(2)}) collective-permute-start(bf16[3,5120]{1,0:T(4,128)(2,1)S(1)} %slice_bitcast_fusion), channel_id=1, source_target_pairs={{0,1},{1,2},{2,3},{3,4},{4,5},{5,6},{6,7},{7,8},{8,9},{9,10},{10,1... | collective-permute-start | bytes 92168 | tf_op jit(solution)/shard_map/ppermute | solution.py:273
  14.1 0.6 copy-start
  132.5 12.6 %collective-permute-start.1 = (bf16[1,128,2048]{2,1,0:T(8,128)(2,1)S(1)}, bf16[1,128,2048]{2,1,0:T(8,128)(2,1)S(1)}, u32[]{:S(2)}, u32[]{:S(2)}) collective-permute-start(bf16[1,128,2048]{2,1,0:T(8,128)(2,1)S(1)} %fusion.5), channel_id=1, source_target_pairs={{0,16},{16,32},{32,48},{48,64},{64,80},{80,96},{96,112},{112,128},... | collective-permute-start | bytes 1572872 | tf_op jit(solution)/shard_map/ppermute | solution.py:280
Sparse Core Ops, SparseCore 0:
  9.3 101.9 all-gather.2

commit v2 on v1

v2 whole, which is shorter than its diff:
```python
import functools

import jax
import jax.numpy as jnp
from jax import lax
from jax.experimental import pallas as pl
from jax.experimental.pallas import tpu as pltpu
from jax.sharding import PartitionSpec as P

HEAD_TOTAL = 8
HK = 128
STEPS = 2
CONV = 4
TOK = 128
PAIR = 2
MESH = pl.DeviceIdType.MESH
highest = lax.Precision.HIGHEST

NN = (((1,), (0,)), ((), ()))
NT = (((1,), (1,)), ((), ()))
TN = (((0,), (0,)), ((), ()))


def split(a):
    high = a.astype(jnp.bfloat16)
    return high, (a - high.astype(jnp.float32)).astype(jnp.bfloat16)


def dot(a, b, dims=NN):
    return lax.dot_general(a, b, dims, preferred_element_type=jnp.float32)


def dot3(a, b, dims=NN):
    (ah, al), (bh, bl) = a, b
    return dot(ah, bh, dims) + (dot(ah, bl, dims) + dot(al, bh, dims))


def unit_rows(vectors):
    return vectors * lax.rsqrt(jnp.sum(vectors * vectors, axis=-1, keepdims=True) + 1e-06)


def local_terms(heads):
    both = STEPS * TOK
    row = lax.broadcasted_iota(jnp.int32, (both, both), 0)
    col = lax.broadcasted_iota(jnp.int32, (both, both), 1)
    row_tok, col_tok = row & (TOK - 1), col & (TOK - 1)
    tok_row = lax.broadcasted_iota(jnp.int32, (TOK, TOK), 0)
    tok_col = lax.broadcasted_iota(jnp.int32, (TOK, TOK), 1)
    before = (col_tok < row_tok) | ((col_tok == row_tok) & (col < row))
    keys, sizes, inner, damp = [], [], [], []
    for q, k0, k1, v0, v1, b0, b1, c_col, c_row in heads:
        key = jnp.concatenate([k0, k1], axis=0)
        keys.append(key)
        sizes.append(jnp.concatenate([b0, b1], axis=0))
        kept = jnp.where(tok_col <= tok_row, jnp.exp(jnp.minimum(c_col - c_row, 0.0)), 0.0)
        damp.append(jnp.concatenate([kept, kept], axis=1))
    key_parts = [split(key) for key in keys]
    lower = []
    for parts, size, kept in zip(key_parts, sizes, damp):
        grid = dot3(parts, parts, NT)
        wide = jnp.concatenate([kept, kept], axis=0)
        lower.append(jnp.where(before, size * wide * grid, 0.0))
    eye = (row == col).astype(jnp.float32)
    same = row_tok == col_tok
    inverse = [eye - jnp.where(same, m, 0.0) for m in lower]
    shift = 0
    while (1 << shift) < TOK:
        joined = ((row_tok >> (shift + 1)) == (col_tok >> (shift + 1))) & (
            (row_tok >> shift) != (col_tok >> shift)
        )
        rounded = [x.astype(jnp.bfloat16) for x in inverse]
        crosses = [jnp.where(joined, m, 0.0).astype(jnp.bfloat16) for m in lower]
        halves = [dot(c, x).astype(jnp.bfloat16) for c, x in zip(crosses, rounded)]
        inverse = [x - dot(p, y) for x, p, y in zip(inverse, rounded, halves)]
        shift += 1
    results = []
    for (q, k0, k1, v0, v1, b0, b1, c_col, c_row), m, parts, kept, x in zip(
        heads, lower, key_parts, damp, inverse
    ):
        grown = jnp.exp(c_col)
        right = jnp.concatenate(
            [
                jnp.concatenate([b0 * v0, b1 * v1], axis=0),
                jnp.concatenate([(b0 * grown) * k0, (b1 * grown) * k1], axis=0),
            ],
            axis=1,
        )
        near = x.astype(jnp.bfloat16)
        solved = dot(near, right.astype(jnp.bfloat16))
        miss = (right - solved) - dot3(split(m), split(solved))
        solved = split(solved + dot(near, miss.astype(jnp.bfloat16)))
        last = c_col[TOK - 1 :, :]
        rest = jnp.exp(last - c_col)
        ends = split(jnp.concatenate([k0 * rest, k1 * rest], axis=0))
        moved = dot3(ends, solved, TN)
        scores = split(dot3(split(q), parts, NT) * kept)
        seen = dot3(scores, solved)
        written, taken = moved[:, :HK], moved[:, HK:]
        direct, reach = seen[:, :HK], q * grown - seen[:, HK:]
        results.append((taken, written, direct, reach, jnp.exp(last)))
    return results


def whole_kernel(
    count, sections,
    rows_ref, taps_ref, beta_ref, gate_ref, gain_ref, w_ref, out_ref,
    ext, rim, taken_hi, taken_lo, reach_hi, reach_lo, written, direct, keep,
    entering, leaving, ready, arrived, gathered,
    rim_sems, w_sems, send_sem, recv_sem, ready_send, ready_recv,
    back_send, back_recv, fore_send, fore_recv,
):
    mine, section = lax.axis_index("ctx"), lax.axis_index("section")
    after, prior = lax.rem(mine + 1, count), lax.rem(mine + count - 1, count)
    onward, behind = lax.rem(section + 1, sections), lax.rem(section + sections - 1, sections)
    fore_steps = (count - 1) // 3
    back_steps = count - 1 - fore_steps
    half_rows = w_ref.shape[0] // 2

    def remote(source, target, sends, receives, **where):
        return pltpu.make_async_remote_copy(
            src_ref=source, dst_ref=target, send_sem=sends, recv_sem=receives,
            device_id=where, device_id_type=MESH,
        )

    barrier = pltpu.get_barrier_semaphore()
    for where in ({"ctx": after}, {"ctx": prior}, {"section": onward}, {"section": behind}):
        pl.semaphore_signal(barrier, inc=1, device_id=where, device_id_type=MESH)
    pl.semaphore_wait(barrier, 4)

    edge = remote(rows_ref.at[TOK - 16 :], rim, rim_sems.at[0], rim_sems.at[1], ctx=after)
    own = remote(w_ref, gathered.at[mine], w_sems.at[0], w_sems.at[1], section=onward)

    @pl.when(mine < count - 1)
    def _():
        edge.start()

    own.start()

    def ring(send, receive, step, half, owner, target):
        block = gathered.at[owner, pl.ds(pl.multiple_of(half * half_rows, half_rows), half_rows)]
        return remote(block, block, send.at[step, half], receive.at[step, half], ctx=target)

    def back(step, half):
        return ring(back_send, back_recv, step, half, lax.rem(mine + step, count), prior)

    def fore(step, half):
        return ring(fore_send, fore_recv, step, half, lax.rem(mine + count - step, count), after)

    def relay(at, carry):
        step, half = lax.div(at, 2), lax.rem(at, 2)
        back(step - 1, half).wait_recv()
        back(step, half).start()

        @pl.when(step < fore_steps)
        def _():
            fore(step - 1, half).wait_recv()
            fore(step, half).start()

        return carry

    tok_row = lax.broadcasted_iota(jnp.int32, (TOK, TOK), 0)
    tok_col = lax.broadcasted_iota(jnp.int32, (TOK, TOK), 1)
    ones = (tok_col <= tok_row).astype(jnp.float32)
    eye = (tok_col == tok_row).astype(jnp.float32)
    gates = gate_ref[...]

    def exact(a, b):
        return lax.dot_general(a, b, NT, precision=highest, preferred_element_type=jnp.float32)

    c_cols, c_rows = exact(ones, gates), exact(gates, ones)
    betas = exact(eye, jax.nn.sigmoid(beta_ref[...]))

    def column(values, which):
        lane = lax.broadcasted_iota(jnp.int32, values.shape, 1)
        return jnp.sum(jnp.where(lane == which, values, 0.0), axis=1, keepdims=True)

    def picked_row(values, which):
        lane = lax.broadcasted_iota(jnp.int32, values.shape, 0)
        return jnp.sum(jnp.where(lane == which, values, 0.0), axis=0, keepdims=True)

    @pl.when(mine == 0)
    def _():
        rim[...] = jnp.zeros_like(rim)
        entering[...] = jnp.zeros_like(entering)

    @pl.when(mine > 0)
    def _():
        edge.wait_recv()

    width = PAIR * HK

    def group(g, carry):
        first = g * PAIR

        def act(n):
            at = pl.ds(pl.multiple_of(n * (HEAD_TOTAL * HK) + g * width, width), width)
            ext[:8, :] = rim[8:, at].astype(jnp.float32)
            ext[8:, :] = rows_ref[:, at].astype(jnp.float32)
            summed = jnp.zeros((TOK, width), jnp.float32)
            taps = taps_ref[:, at].astype(jnp.float32)
            for i in range(CONV):
                start = 8 - (CONV - 1) + i
                summed = summed + taps[i : i + 1] * ext[start : start + TOK, :]
            return summed * jax.nn.sigmoid(summed)

        queries, key_0, key_1, value_0, value_1 = [act(n) for n in range(1 + 2 * STEPS)]
        heads = []
        for p in range(PAIR):
            at = slice(p * HK, (p + 1) * HK)
            heads.append(
                (
                    unit_rows(queries[:, at]),
                    unit_rows(key_0[:, at]),
                    unit_rows(key_1[:, at]),
                    value_0[:, at],
                    value_1[:, at],
                    column(betas, first + p),
                    column(betas, HEAD_TOTAL + first + p),
                    column(c_cols, first + p),
                    picked_row(c_rows, first + p),
                )
            )
        for p, (took, wrote, seen, reach, kept) in enumerate(local_terms(heads)):
            h = first + p
            taken_hi[h], taken_lo[h] = split(took)
            reach_hi[h], reach_lo[h] = split(reach)
            written[h] = wrote
            direct[h] = seen
            keep[h] = jnp.broadcast_to(kept, (8, HK))

        @pl.when(g == 0)
        def _():
            own.wait_recv()
            for half in range(2):
                back(0, half).start()
                fore(0, half).start()

        return carry

    lax.fori_loop(0, HEAD_TOTAL // PAIR, group, 0)

    lead = jnp.minimum(4 + 2 * lax.div(mine, 2), 2 * back_steps)
    lax.fori_loop(2, lead, relay, 0)

    def hop(h):
        return remote(leaving.at[h], entering.at[h], send_sem.at[h], recv_sem.at[h], ctx=after)

    def share(h):
        return remote(ready.at[h], arrived.at[h], ready_send.at[h], ready_recv.at[h], section=onward)

    for h in range(HEAD_TOTAL):
        @pl.when(mine > 0)
        def _():
            hop(h).wait_recv()

        state = entering[h]
        parts = split(state)

        @pl.when(mine < count - 1)
        def _():
            step = dot3((taken_hi[h], taken_lo[h]), parts)
            leaving[h] = (keep[h][:1] * state + written[h]) - step
            hop(h).start()

        made = direct[h] + dot3((reach_hi[h], reach_lo[h]), parts)
        scale = lax.rsqrt(jnp.mean(made * made, axis=-1, keepdims=True) + 1e-05)
        gain = gain_ref[:, h * HK : (h + 1) * HK]
        ready[h] = (made * scale * gain).astype(jnp.bfloat16)
        share(h).start()

    lax.fori_loop(lead, 2 * back_steps, relay, 0)
    for half in range(2):
        back(back_steps - 1, half).wait_recv()
        fore(fore_steps - 1, half).wait_recv()
    for h in range(HEAD_TOTAL):
        share(h).wait_recv()
    normed = jnp.concatenate([arrived[h] for h in range(HEAD_TOTAL)], axis=1)

    def columns(n, carry):
        block = jnp.concatenate([gathered[2 * n], gathered[2 * n + 1]], axis=1)
        wide = block.shape[1]
        out_ref[:, pl.ds(pl.multiple_of(n * wide, wide), wide)] = dot(normed, block).astype(
            jnp.bfloat16
        )
        return carry

    lax.fori_loop(0, count // 2, columns, 0)

    own.wait_send()

    @pl.when(mine < count - 1)
    def _():
        edge.wait_send()
        for h in range(HEAD_TOTAL):
            hop(h).wait_send()

    for h in range(HEAD_TOTAL):
        share(h).wait_send()
    for half in range(2):
        for step in range(back_steps):
            back(step, half).wait_send()
        for step in range(fore_steps):
            fore(step, half).wait_send()


def on_device(streams, conv_weight, beta_logit, gate_log, norm_gain, w_out):
    count, sections = lax.axis_size("ctx"), lax.axis_size("section")
    fore_steps = (count - 1) // 3
    back_steps = count - 1 - fore_steps
    heads = (HEAD_TOTAL, HK, HK)
    depth, share = w_out.shape[1:]
    whole = pl.BlockSpec(memory_space=pltpu.VMEM)
    dma = pltpu.SemaphoreType.DMA
    mixed = pl.pallas_call(
        functools.partial(whole_kernel, count, sections),
        in_specs=[whole] * 6,
        out_specs=whole,
        out_shape=jax.ShapeDtypeStruct((TOK, count * share), jnp.bfloat16),
        scratch_shapes=[
            pltpu.VMEM((TOK + 8, PAIR * HK), jnp.float32),
            pltpu.VMEM((16, streams.shape[2]), jnp.bfloat16),
            pltpu.VMEM(heads, jnp.bfloat16),
            pltpu.VMEM(heads, jnp.bfloat16),
            pltpu.VMEM(heads, jnp.bfloat16),
            pltpu.VMEM(heads, jnp.bfloat16),
            pltpu.VMEM(heads, jnp.float32),
            pltpu.VMEM(heads, jnp.float32),
            pltpu.VMEM((HEAD_TOTAL, 8, HK), jnp.float32),
            pltpu.VMEM(heads, jnp.float32),
            pltpu.VMEM(heads, jnp.float32),
            pltpu.VMEM(heads, jnp.bfloat16),
            pltpu.VMEM(heads, jnp.bfloat16),
            pltpu.VMEM((count, depth, share), jnp.bfloat16),
            dma((2,)),
            dma((2,)),
            dma((HEAD_TOTAL,)),
            dma((HEAD_TOTAL,)),
            dma((HEAD_TOTAL,)),
            dma((HEAD_TOTAL,)),
            dma((back_steps, 2)),
            dma((back_steps, 2)),
            dma((fore_steps, 2)),
            dma((fore_steps, 2)),
        ],
        compiler_params=pltpu.CompilerParams(
            collective_id=0, has_side_effects=True, vmem_limit_bytes=60 * 2**20
        ),
        name="whole_mixer",
    )(streams[0], conv_weight[0], beta_logit[0].T, gate_log[0].T, norm_gain, w_out[0])
    return mixed[None]


def solution(mesh):
    placed = (
        P("section", "ctx", None),
        P("section", None, None),
        P("section", "ctx", None),
        P("section", "ctx", None),
        P("section", None),
        P("section", None, "ctx"),
    )
    return jax.shard_map(
        on_device, mesh=mesh, in_specs=placed, out_specs=P("section", "ctx", None), check_vma=False
    )
```

time: 153 us -> 111 us (0.73)
  the two profiles are of different devices: /device:TPU:496 before, /device:TPU:448 now
where the time goes in v2:
time: 111 us
  Pallas kernels  109 us (98%)
  local copies, waits for them, and re-layouts  1.88 us (2%)
    pallas_call x1, Pallas kernels, on_device(): pl.pallas_call(functools.partial(whole_kernel, count, sections), in_specs...  109 us

profile of v2, /device:TPU:448, one launch (start us, length us, event | category | flops | bytes accessed | tf_op | source)
XLA Modules:
  0.0 110.7 jit_solution(1084640004052552010)
XLA Ops:
  0.0 108.8 %whole_mixer.1 = bf16[128,2048]{1,0:T(8,128)(2,1)} custom-call(bf16[128,5120]{1,0:T(8,128)(2,1)} %bitcast.11, bf16[4,5120]{1,0:T(4,128)(2,1)} %bitcast.13, f32[16,128]{1,0:T(8,128)} %bitcast.14, f32[8,128]{1,0:T(8,128)} %bitcast.15, f32[1,1024]{1,0:T(1,128)} %gain_ref.1, bf16[1024,128]{1,0:T(8,128)(2,1)} %bitcast.12), custom_call_target="tpu_custom_call" | custom-call | tf_op jit(solution)/shard_map/whole_mixer/pallas_call | solution.py:314
  108.8 1.9 %copy.8 = bf16[1,128,2048]{2,1,0:T(8,128)(2,1)} copy(bf16[1,128,2048]{2,1,0:T(8,128)(2,1)} %bitcast.10) | data formatting | bytes 1048576

commit v3 on v2

--- a/solution.py
+++ b/solution.py
@@ -40,63 +40,85 @@
 
 
 def local_terms(heads):
-    both = STEPS * TOK
-    row = lax.broadcasted_iota(jnp.int32, (both, both), 0)
-    col = lax.broadcasted_iota(jnp.int32, (both, both), 1)
-    row_tok, col_tok = row & (TOK - 1), col & (TOK - 1)
-    tok_row = lax.broadcasted_iota(jnp.int32, (TOK, TOK), 0)
-    tok_col = lax.broadcasted_iota(jnp.int32, (TOK, TOK), 1)
-    before = (col_tok < row_tok) | ((col_tok == row_tok) & (col < row))
-    keys, sizes, inner, damp = [], [], [], []
+    half = TOK // 2
+    row = lax.broadcasted_iota(jnp.int32, (TOK, TOK), 0)
+    col = lax.broadcasted_iota(jnp.int32, (TOK, TOK), 1)
+    row_tok, col_tok = row & (half - 1), col & (half - 1)
+    same = row_tok == col_tok
+    before = (col_tok < row_tok) | (same & (col < row))
+    eye = (row == col).astype(jnp.float32)
+
+    def halves(first, second):
+        return [
+            jnp.concatenate([first[at : at + half], second[at : at + half]], axis=0)
+            for at in (0, half)
+        ]
+
+    keys, sizes, cols, rows, grids = [], [], [], [], []
     for q, k0, k1, v0, v1, b0, b1, c_col, c_row in heads:
-        key = jnp.concatenate([k0, k1], axis=0)
-        keys.append(key)
-        sizes.append(jnp.concatenate([b0, b1], axis=0))
-        kept = jnp.where(tok_col <= tok_row, jnp.exp(jnp.minimum(c_col - c_row, 0.0)), 0.0)
-        damp.append(jnp.concatenate([kept, kept], axis=1))
-    key_parts = [split(key) for key in keys]
-    lower = []
-    for parts, size, kept in zip(key_parts, sizes, damp):
-        grid = dot3(parts, parts, NT)
-        wide = jnp.concatenate([kept, kept], axis=0)
-        lower.append(jnp.where(before, size * wide * grid, 0.0))
-    eye = (row == col).astype(jnp.float32)
-    same = row_tok == col_tok
+        keys.append([split(part) for part in halves(k0, k1)])
+        sizes.append(halves(b0, b1))
+        cols.append(halves(c_col, c_col))
+        rows.append(
+            [jnp.concatenate([c_row[:, at : at + half]] * 2, axis=1) for at in (0, half)]
+        )
+        (early, late) = keys[-1]
+        grids.append((dot3(early, early, NT), dot3(late, late, NT), dot3(late, early, NT)))
+
+    def faded(n, i, j, grid):
+        return sizes[n][i] * jnp.exp(jnp.minimum(cols[n][i] - rows[n][j], 0.0)) * grid
+
+    lower, below = [], []
+    for n, (first, second, cross) in enumerate(grids):
+        lower.append(jnp.where(before, faded(n, 0, 0, first), 0.0))
+        lower.append(jnp.where(before, faded(n, 1, 1, second), 0.0))
+        below.append(split(faded(n, 1, 0, cross)))
     inverse = [eye - jnp.where(same, m, 0.0) for m in lower]
     shift = 0
-    while (1 << shift) < TOK:
+    while (1 << shift) < half:
         joined = ((row_tok >> (shift + 1)) == (col_tok >> (shift + 1))) & (
             (row_tok >> shift) != (col_tok >> shift)
         )
         rounded = [x.astype(jnp.bfloat16) for x in inverse]
         crosses = [jnp.where(joined, m, 0.0).astype(jnp.bfloat16) for m in lower]
-        halves = [dot(c, x).astype(jnp.bfloat16) for c, x in zip(crosses, rounded)]
-        inverse = [x - dot(p, y) for x, p, y in zip(inverse, rounded, halves)]
+        products = [dot(c, x).astype(jnp.bfloat16) for c, x in zip(crosses, rounded)]
+        inverse = [x - dot(p, y) for x, p, y in zip(inverse, rounded, products)]
         shift += 1
+    near = [x.astype(jnp.bfloat16) for x in inverse]
+    lower = [split(m) for m in lower]
+
+    def solve(ms, xs, sides):
+        got = [dot(x, side.astype(jnp.bfloat16)) for x, side in zip(xs, sides)]
+        miss = [(side - s) - dot3(m, split(s)) for side, s, m in zip(sides, got, ms)]
+        return [split(s + dot(x, e.astype(jnp.bfloat16))) for s, x, e in zip(got, xs, miss)]
+
+    sides = []
+    for n, (q, k0, k1, v0, v1, b0, b1, c_col, c_row) in enumerate(heads):
+        grown = jnp.exp(c_col)
+        values, scaled = halves(b0 * v0, b1 * v1), halves((b0 * grown) * k0, (b1 * grown) * k1)
+        sides.append([jnp.concatenate([v, k], axis=1) for v, k in zip(values, scaled)])
+    tops = solve(lower[::2], near[::2], [side[0] for side in sides])
+    bottoms = solve(
+        lower[1::2],
+        near[1::2],
+        [side[1] - dot3(m, top) for side, m, top in zip(sides, below, tops)],
+    )
+    score_col = lax.broadcasted_iota(jnp.int32, (TOK, STEPS * TOK), 1)
+    score_tok = (score_col // TOK) * half + (score_col & (half - 1))
+    allowed = score_tok <= lax.broadcasted_iota(jnp.int32, (TOK, STEPS * TOK), 0)
     results = []
-    for (q, k0, k1, v0, v1, b0, b1, c_col, c_row), m, parts, kept, x in zip(
-        heads, lower, key_parts, damp, inverse
-    ):
-        grown = jnp.exp(c_col)
-        right = jnp.concatenate(
-            [
-                jnp.concatenate([b0 * v0, b1 * v1], axis=0),
-                jnp.concatenate([(b0 * grown) * k0, (b1 * grown) * k1], axis=0),
-            ],
-            axis=1,
-        )
-        near = x.astype(jnp.bfloat16)
-        solved = dot(near, right.astype(jnp.bfloat16))
-        miss = (right - solved) - dot3(split(m), split(solved))
-        solved = split(solved + dot(near, miss.astype(jnp.bfloat16)))
+    for n, (q, k0, k1, v0, v1, b0, b1, c_col, c_row) in enumerate(heads):
+        solved = [jnp.concatenate(pair, axis=0) for pair in zip(tops[n], bottoms[n])]
         last = c_col[TOK - 1 :, :]
         rest = jnp.exp(last - c_col)
-        ends = split(jnp.concatenate([k0 * rest, k1 * rest], axis=0))
+        ends = split(jnp.concatenate(halves(k0 * rest, k1 * rest), axis=0))
         moved = dot3(ends, solved, TN)
-        scores = split(dot3(split(q), parts, NT) * kept)
+        both = [jnp.concatenate(pair, axis=0) for pair in zip(*keys[n])]
+        fade = jnp.exp(jnp.minimum(c_col - jnp.concatenate(rows[n], axis=1), 0.0))
+        scores = split(jnp.where(allowed, dot3(split(q), both, NT) * fade, 0.0))
         seen = dot3(scores, solved)
         written, taken = moved[:, :HK], moved[:, HK:]
-        direct, reach = seen[:, :HK], q * grown - seen[:, HK:]
+        direct, reach = seen[:, :HK], q * jnp.exp(c_col) - seen[:, HK:]
         results.append((taken, written, direct, reach, jnp.exp(last)))
     return results
 
@@ -188,6 +210,38 @@
         edge.wait_recv()
 
     width = PAIR * HK
+    groups = HEAD_TOTAL // PAIR
+
+    def hop(h):
+        return remote(leaving.at[h], entering.at[h], send_sem.at[h], recv_sem.at[h], ctx=after)
+
+    def share(h):
+        return remote(ready.at[h], arrived.at[h], ready_send.at[h], ready_recv.at[h], section=onward)
+
+    def chain(h):
+        @pl.when(mine > 0)
+        def _():
+            hop(h).wait_recv()
+
+        state = entering[h]
+        parts = split(state)
+
+        @pl.when(mine < count - 1)
+        def _():
+            step = dot3((taken_hi[h], taken_lo[h]), parts)
+            leaving[h] = (keep[h][:1] * state + written[h]) - step
+            hop(h).start()
+
+        made = direct[h] + dot3((reach_hi[h], reach_lo[h]), parts)
+        scale = lax.rsqrt(jnp.mean(made * made, axis=-1, keepdims=True) + 1e-05)
+        gain = gain_ref[:, pl.ds(pl.multiple_of(h * HK, HK), HK)]
+        ready[h] = (made * scale * gain).astype(jnp.bfloat16)
+        share(h).start()
+
+    def chain_group(g, carry):
+        for p in range(PAIR):
+            chain(g * PAIR + p)
+        return carry
 
     def group(g, carry):
         first = g * PAIR
@@ -235,38 +289,23 @@
                 back(0, half).start()
                 fore(0, half).start()
 
+        @pl.when(g > 0)
+        def _():
+            for half in range(2):
+                relay(2 * g + half, 0)
+
+        @pl.when(g >= mine)
+        def _():
+            chain_group(g - mine, 0)
+
         return carry
 
-    lax.fori_loop(0, HEAD_TOTAL // PAIR, group, 0)
-
-    lead = jnp.minimum(4 + 2 * lax.div(mine, 2), 2 * back_steps)
-    lax.fori_loop(2, lead, relay, 0)
-
-    def hop(h):
-        return remote(leaving.at[h], entering.at[h], send_sem.at[h], recv_sem.at[h], ctx=after)
-
-    def share(h):
-        return remote(ready.at[h], arrived.at[h], ready_send.at[h], ready_recv.at[h], section=onward)
-
-    for h in range(HEAD_TOTAL):
-        @pl.when(mine > 0)
-        def _():
-            hop(h).wait_recv()
-
-        state = entering[h]
-        parts = split(state)
-
-        @pl.when(mine < count - 1)
-        def _():
-            step = dot3((taken_hi[h], taken_lo[h]), parts)
-            leaving[h] = (keep[h][:1] * state + written[h]) - step
-            hop(h).start()
-
-        made = direct[h] + dot3((reach_hi[h], reach_lo[h]), parts)
-        scale = lax.rsqrt(jnp.mean(made * made, axis=-1, keepdims=True) + 1e-05)
-        gain = gain_ref[:, h * HK : (h + 1) * HK]
-        ready[h] = (made * scale * gain).astype(jnp.bfloat16)
-        share(h).start()
+    lax.fori_loop(0, groups, group, 0)
+
+    lead = jnp.minimum(2 * groups + 2 * lax.div(mine, 2), 2 * back_steps)
+    lax.fori_loop(2 * groups, lead, relay, 0)
+
+    lax.fori_loop(jnp.maximum(groups - mine, 0), groups, chain_group, 0)
 
     lax.fori_loop(lead, 2 * back_steps, relay, 0)
     for half in range(2):

time: 111 us -> 105 us (0.946)
  the two profiles are of different devices: /device:TPU:448 before, /device:TPU:481 now
where the time goes in v3:
time: 105 us
  Pallas kernels  103 us (98%)
  local copies, waits for them, and re-layouts  1.88 us (2%)
    pallas_call x1, Pallas kernels, on_device(): pl.pallas_call(functools.partial(whole_kernel, count, sections), in_specs...  103 us

profile of v3, /device:TPU:481, one launch (start us, length us, event | category | flops | bytes accessed | tf_op | source)
XLA Modules:
  0.0 104.8 jit_solution(1307941107130770471)
XLA Ops:
  0.0 102.9 %whole_mixer.1 = bf16[128,2048]{1,0:T(8,128)(2,1)} custom-call(bf16[128,5120]{1,0:T(8,128)(2,1)} %bitcast.11, bf16[4,5120]{1,0:T(4,128)(2,1)} %bitcast.13, f32[16,128]{1,0:T(8,128)} %bitcast.14, f32[8,128]{1,0:T(8,128)} %bitcast.15, f32[1,1024]{1,0:T(1,128)} %gain_ref.1, bf16[1024,128]{1,0:T(8,128)(2,1)} %bitcast.12), custom_call_target="tpu_custom_call" | custom-call | tf_op jit(solution)/shard_map/whole_mixer/pallas_call | solution.py:353
  102.9 1.9 %copy.8 = bf16[1,128,2048]{2,1,0:T(8,128)(2,1)} copy(bf16[1,128,2048]{2,1,0:T(8,128)(2,1)} %bitcast.10) | data formatting | bytes 1048576

commit v4 on v3

--- a/solution.py
+++ b/solution.py
@@ -112,12 +112,12 @@
         last = c_col[TOK - 1 :, :]
         rest = jnp.exp(last - c_col)
         ends = split(jnp.concatenate(halves(k0 * rest, k1 * rest), axis=0))
-        moved = dot3(ends, solved, TN)
+        moved = dot3(solved, ends, TN)
         both = [jnp.concatenate(pair, axis=0) for pair in zip(*keys[n])]
         fade = jnp.exp(jnp.minimum(c_col - jnp.concatenate(rows[n], axis=1), 0.0))
         scores = split(jnp.where(allowed, dot3(split(q), both, NT) * fade, 0.0))
         seen = dot3(scores, solved)
-        written, taken = moved[:, :HK], moved[:, HK:]
+        written, taken = moved[:HK], moved[HK:]
         direct, reach = seen[:, :HK], q * jnp.exp(c_col) - seen[:, HK:]
         results.append((taken, written, direct, reach, jnp.exp(last)))
     return results
@@ -212,27 +212,32 @@
     width = PAIR * HK
     groups = HEAD_TOTAL // PAIR
 
-    def hop(h):
-        return remote(leaving.at[h], entering.at[h], send_sem.at[h], recv_sem.at[h], ctx=after)
+    def hop(h, part):
+        at = pl.ds(part * (HK // 2), HK // 2)
+        return remote(
+            leaving.at[h, at], entering.at[h, at], send_sem.at[h, part], recv_sem.at[h, part], ctx=after
+        )
 
     def share(h):
         return remote(ready.at[h], arrived.at[h], ready_send.at[h], ready_recv.at[h], section=onward)
 
     def chain(h):
-        @pl.when(mine > 0)
-        def _():
-            hop(h).wait_recv()
-
-        state = entering[h]
-        parts = split(state)
-
-        @pl.when(mine < count - 1)
-        def _():
-            step = dot3((taken_hi[h], taken_lo[h]), parts)
-            leaving[h] = (keep[h][:1] * state + written[h]) - step
-            hop(h).start()
-
-        made = direct[h] + dot3((reach_hi[h], reach_lo[h]), parts)
+        moves = (taken_hi[h], taken_lo[h])
+        for part in range(2):
+            at = slice(part * (HK // 2), (part + 1) * (HK // 2))
+
+            @pl.when(mine > 0)
+            def _():
+                hop(h, part).wait_recv()
+
+            @pl.when(mine < count - 1)
+            def _():
+                state = entering[h, at]
+                step = dot3(split(state), moves)
+                leaving[h, at] = (keep[h][:1] * state + written[h, at]) - step
+                hop(h, part).start()
+
+        made = direct[h] + dot3((reach_hi[h], reach_lo[h]), split(entering[h]), NT)
         scale = lax.rsqrt(jnp.mean(made * made, axis=-1, keepdims=True) + 1e-05)
         gain = gain_ref[:, pl.ds(pl.multiple_of(h * HK, HK), HK)]
         ready[h] = (made * scale * gain).astype(jnp.bfloat16)
@@ -289,10 +294,10 @@
                 back(0, half).start()
                 fore(0, half).start()
 
-        @pl.when(g > 0)
+        @pl.when(g > 1)
         def _():
             for half in range(2):
-                relay(2 * g + half, 0)
+                relay(2 * (g - 1) + half, 0)
 
         @pl.when(g >= mine)
         def _():
@@ -302,12 +307,23 @@
 
     lax.fori_loop(0, groups, group, 0)
 
-    lead = jnp.minimum(2 * groups + 2 * lax.div(mine, 2), 2 * back_steps)
-    lax.fori_loop(2 * groups, lead, relay, 0)
-
-    lax.fori_loop(jnp.maximum(groups - mine, 0), groups, chain_group, 0)
-
-    lax.fori_loop(lead, 2 * back_steps, relay, 0)
+    ring_end = 2 * back_steps
+    begin = 2 * (groups - 1)
+    lead = jnp.minimum(begin + lax.div(2 * mine, 3), ring_end)
+    lax.fori_loop(begin, lead, relay, 0)
+    late = jnp.maximum(groups - mine, 0)
+
+    def chain_and_ring(g, carry):
+        chain_group(g, 0)
+
+        @pl.when(lead + g - late < ring_end)
+        def _():
+            relay(lead + g - late, 0)
+
+        return carry
+
+    lax.fori_loop(late, groups, chain_and_ring, 0)
+    lax.fori_loop(jnp.minimum(lead + groups - late, ring_end), ring_end, relay, 0)
     for half in range(2):
         back(back_steps - 1, half).wait_recv()
         fore(fore_steps - 1, half).wait_recv()
@@ -331,7 +347,8 @@
     def _():
         edge.wait_send()
         for h in range(HEAD_TOTAL):
-            hop(h).wait_send()
+            for part in range(2):
+                hop(h, part).wait_send()
 
     for h in range(HEAD_TOTAL):
         share(h).wait_send()
@@ -372,8 +389,8 @@
             pltpu.VMEM((count, depth, share), jnp.bfloat16),
             dma((2,)),
             dma((2,)),
-            dma((HEAD_TOTAL,)),
-            dma((HEAD_TOTAL,)),
+            dma((HEAD_TOTAL, 2)),
+            dma((HEAD_TOTAL, 2)),
             dma((HEAD_TOTAL,)),
             dma((HEAD_TOTAL,)),
             dma((back_steps, 2)),

time: 105 us -> 101 us (0.962)
  the two profiles are of different devices: /device:TPU:481 before, /device:TPU:476 now
where the time goes in v4:
time: 101 us
  Pallas kernels  99.1 us (98%)
  local copies, waits for them, and re-layouts  1.88 us (2%)
    pallas_call x1, Pallas kernels, on_device(): pl.pallas_call(functools.partial(whole_kernel, count, sections), in_specs...  99.1 us

profile of v4, /device:TPU:476, one launch (start us, length us, event | category | flops | bytes accessed | tf_op | source)
XLA Modules:
  0.0 101.0 jit_solution(15378133710166872124)
XLA Ops:
  0.0 99.1 %whole_mixer.1 = bf16[128,2048]{1,0:T(8,128)(2,1)} custom-call(bf16[128,5120]{1,0:T(8,128)(2,1)} %bitcast.11, bf16[4,5120]{1,0:T(4,128)(2,1)} %bitcast.13, f32[16,128]{1,0:T(8,128)} %bitcast.14, f32[8,128]{1,0:T(8,128)} %bitcast.15, f32[1,1024]{1,0:T(1,128)} %gain_ref.1, bf16[1024,128]{1,0:T(8,128)(2,1)} %bitcast.12), custom_call_target="tpu_custom_call" | custom-call | tf_op jit(solution)/shard_map/whole_mixer/pallas_call | solution.py:370
  99.1 1.9 %copy.8 = bf16[1,128,2048]{2,1,0:T(8,128)(2,1)} copy(bf16[1,128,2048]{2,1,0:T(8,128)(2,1)} %bitcast.10) | data formatting | bytes 1048576

commit v5 on v4

--- a/solution.py
+++ b/solution.py
@@ -127,14 +127,14 @@
     count, sections,
     rows_ref, taps_ref, beta_ref, gate_ref, gain_ref, w_ref, out_ref,
     ext, rim, taken_hi, taken_lo, reach_hi, reach_lo, written, direct, keep,
-    entering, leaving, ready, arrived, gathered,
+    entering, leaving, ready, arrived, gathered, total,
     rim_sems, w_sems, send_sem, recv_sem, ready_send, ready_recv,
     back_send, back_recv, fore_send, fore_recv,
 ):
     mine, section = lax.axis_index("ctx"), lax.axis_index("section")
     after, prior = lax.rem(mine + 1, count), lax.rem(mine + count - 1, count)
     onward, behind = lax.rem(section + 1, sections), lax.rem(section + sections - 1, sections)
-    fore_steps = (count - 1) // 3
+    fore_steps = 2 * (count - 1) // 5
     back_steps = count - 1 - fore_steps
     half_rows = w_ref.shape[0] // 2
 
@@ -327,19 +327,30 @@
     for half in range(2):
         back(back_steps - 1, half).wait_recv()
         fore(fore_steps - 1, half).wait_recv()
-    for h in range(HEAD_TOTAL):
-        share(h).wait_recv()
-    normed = jnp.concatenate([arrived[h] for h in range(HEAD_TOTAL)], axis=1)
-
-    def columns(n, carry):
-        block = jnp.concatenate([gathered[2 * n], gathered[2 * n + 1]], axis=1)
-        wide = block.shape[1]
-        out_ref[:, pl.ds(pl.multiple_of(n * wide, wide), wide)] = dot(normed, block).astype(
-            jnp.bfloat16
-        )
-        return carry
-
-    lax.fori_loop(0, count // 2, columns, 0)
+    early = HEAD_TOTAL - PAIR
+
+    def product(heads, finish):
+        for h in heads:
+            share(h).wait_recv()
+        normed = jnp.concatenate([arrived[h] for h in heads], axis=1)
+        rows = slice(heads[0] * HK, (heads[-1] + 1) * HK)
+
+        def columns(n, carry):
+            block = jnp.concatenate([gathered[2 * n, rows], gathered[2 * n + 1, rows]], axis=1)
+            wide = block.shape[1]
+            finish(pl.ds(pl.multiple_of(n * wide, wide), wide), dot(normed, block))
+            return carry
+
+        lax.fori_loop(0, count // 2, columns, 0)
+
+    def hold(at, part):
+        total[:, at] = part
+
+    def close(at, part):
+        out_ref[:, at] = (total[:, at] + part).astype(jnp.bfloat16)
+
+    product(range(early), hold)
+    product(range(early, HEAD_TOTAL), close)
 
     own.wait_send()
 
@@ -361,7 +372,7 @@
 
 def on_device(streams, conv_weight, beta_logit, gate_log, norm_gain, w_out):
     count, sections = lax.axis_size("ctx"), lax.axis_size("section")
-    fore_steps = (count - 1) // 3
+    fore_steps = 2 * (count - 1) // 5
     back_steps = count - 1 - fore_steps
     heads = (HEAD_TOTAL, HK, HK)
     depth, share = w_out.shape[1:]
@@ -387,6 +398,7 @@
             pltpu.VMEM(heads, jnp.bfloat16),
             pltpu.VMEM(heads, jnp.bfloat16),
             pltpu.VMEM((count, depth, share), jnp.bfloat16),
+            pltpu.VMEM((TOK, count * share), jnp.float32),
             dma((2,)),
             dma((2,)),
             dma((HEAD_TOTAL, 2)),

time: 101 us -> 100 us (0.990)
  the two profiles are of different devices: /device:TPU:476 before, /device:TPU:481 now
where the time goes in v5:
time: 100 us; the launch traced here: 99.1 us
  Pallas kernels  97.2 us (97%)
  local copies, waits for them, and re-layouts  1.88 us (2%)
    pallas_call x1, Pallas kernels, on_device(): pl.pallas_call(functools.partial(whole_kernel, count, sections), in_specs...  97.2 us

profile of v5, /device:TPU:481, one launch (start us, length us, event | category | flops | bytes accessed | tf_op | source)
XLA Modules:
  0.0 99.1 jit_solution(14677627773612523224)
XLA Ops:
  0.0 97.2 %whole_mixer.1 = bf16[128,2048]{1,0:T(8,128)(2,1)} custom-call(bf16[128,5120]{1,0:T(8,128)(2,1)} %bitcast.11, bf16[4,5120]{1,0:T(4,128)(2,1)} %bitcast.13, f32[16,128]{1,0:T(8,128)} %bitcast.14, f32[8,128]{1,0:T(8,128)} %bitcast.15, f32[1,1024]{1,0:T(1,128)} %gain_ref.1, bf16[1024,128]{1,0:T(8,128)(2,1)} %bitcast.12), custom_call_target="tpu_custom_call" | custom-call | tf_op jit(solution)/shard_map/whole_mixer/pallas_call | solution.py:381
  97.2 1.9 %copy.8 = bf16[1,128,2048]{2,1,0:T(8,128)(2,1)} copy(bf16[1,128,2048]{2,1,0:T(8,128)(2,1)} %bitcast.10) | data formatting | bytes 1048576
